TPU v7x, 128 devices: a whole 4x4x4 slice. The times are simulated.
128 devices in a mesh: shell: 16 (over z, x), blk: 8 (over y, core).
Axes of the slice: x: 4, y: 4, z: 4, core: 2. Of those that a mesh axis runs over, the one named last changes fastest.
Arguments:
- cycle_fourier: bfloat16 [512, 2, 192, 1024], P('shell', None, None, 'blk'), may hold values from -6 to 6
- legendre: bfloat16 [192, 768, 1024], P('shell', None, 'blk'), may hold values from -0.1875 to 0.1875
- azimuth_orders: int32 [192], replicated, may hold values from 0 to 767, as said below
- multipole: int32 [768], P(('shell', 'blk')), may hold values from 0 to 767, each once
- bessel: bfloat16 [768, 512, 512], P(('shell', 'blk')), may hold values from -0.25 to 0.25
- signal_power: float32 [768, 512], P(('shell', 'blk')), may hold values from 0.1 to 10
- noise_power: float32 [768, 512], P(('shell', 'blk')), may hold values from 0.1 to 10
Outputs:
- filtered: bfloat16 [768, 512, 384], P('shell', 'blk')
Inputs may be any that keep to these rules, and one draw needn't show every extreme that they name: `azimuth_orders`: distinct orders; 0 and 767 always among them. Each multipole 0 to 767 appears once.
All inputs are finite; a program needn't handle non-finite values.
Results may differ from a plain program's by a relative error of at most 0.017.
Values may be sent and summed in bfloat16 or wider, within the bound.
A program may use at most 128 MiB of HBM per device.

v0:
```python
import jax
import jax.numpy as jnp
from jax import lax
from jax.sharding import Mesh, PartitionSpec as P

PLANE = ("z", "x", "y")
ALL = ("z", "x", "y", "core")
SHELL = ("z", "x")
BLK = ("y", "core")


def body(cycle_fourier, legendre, azimuth_orders, multipole, bessel, signal_power, noise_power):
    shells, _, cols, cycles = cycle_fourier.shape
    ny = lax.axis_size("y")
    per = cols // (lax.axis_size("z") * lax.axis_size("x") * ny)
    planes = cols // per
    f = cycle_fourier.transpose(2, 1, 0, 3)
    f = lax.all_to_all(f, PLANE, split_axis=0, concat_axis=0, tiled=True)
    f = f.reshape(planes // ny, ny, per, 2, shells, cycles)
    rows = legendre.shape[1]
    t = lax.all_to_all(legendre, "y", split_axis=0, concat_axis=0, tiled=True)
    t = t.reshape(ny, per, rows, cycles)
    part = jnp.einsum("yjir,ayjcsr->cjias", t, f, preferred_element_type=jnp.float32)
    part = part.astype(jnp.bfloat16).reshape(2, per, rows, planes // ny * shells)
    both = lax.all_to_all(part, "core", split_axis=0, concat_axis=0, tiled=True)
    c = (both[0].astype(jnp.float32) + both[1].astype(jnp.float32)).astype(jnp.bfloat16)
    total = c.shape[-1]
    devices = planes * 2
    local = rows // devices
    c = c.reshape(per, devices, local, total).transpose(1, 2, 0, 3)
    c = lax.all_to_all(c, ALL, split_axis=0, concat_axis=0, tiled=True)
    c = c.reshape(planes, 2, local, per, total).transpose(2, 0, 3, 1, 4)
    coeffs = c.reshape(local, cols, 2, total)
    allowed = multipole[:, None] >= azimuth_orders[None, :]
    coeffs = jnp.where(allowed[:, :, None, None], coeffs, jnp.zeros((), jnp.bfloat16))
    coeffs = coeffs.reshape(local, cols * 2, total)
    forward = jnp.einsum("iks,ijs->ikj", bessel, coeffs, preferred_element_type=jnp.float32)
    wiener = signal_power / (signal_power + noise_power)
    scaled = (forward * wiener[:, :, None]).astype(jnp.bfloat16)
    out = jnp.einsum("iks,ikj->isj", bessel, scaled, preferred_element_type=jnp.float32)
    return lax.all_to_all(out.astype(jnp.bfloat16), BLK, split_axis=1, concat_axis=0, tiled=True)


def solution(mesh):
    fine = Mesh(mesh.devices.reshape(4, 4, 4, 2), ALL)
    return jax.shard_map(
        body,
        mesh=fine,
        in_specs=(
            P(SHELL, None, None, BLK),
            P(SHELL, None, BLK),
            P(),
            P(ALL),
            P(ALL, None, None),
            P(ALL, None),
            P(ALL, None),
        ),
        out_specs=P(SHELL, BLK, None),
        check_vma=False,
    )
```

profile of v0, /device:TPU:1, one launch (start us, length us, event | category | flops | bytes accessed | tf_op | source)
XLA Modules:
  0.0 224.5 jit_solution(8660560980968956102)
XLA Ops:
  0.0 0.0 copy-start
  0.0 5.3 %all-to-all-start.1 = ((bf16[12,768,128]{2,1,0:T(8,128)(2,1)}), bf16[12,768,128]{2,1,0:T(8,128)(2,1)}, u32[]{:S(2)}, u32[]{:S(2)}) async-start(bf16[12,768,128]{2,1,0:T(8,128)(2,1)} %param.8), calls=%async_computation.1 | async-start | bytes 4718592 | tf_op jit(solution)/shard_map/all_to_all | solution.py:21
  5.3 5.6 %copy.49 = bf16[32,2,192,128]{3,0,1,2:T(8,128)(2,1)} copy(bf16[32,2,192,128]{3,2,1,0:T(8,128)(2,1)} %param.7) | data formatting | bytes 6291456 | tf_op args[0]
  10.8 23.3 %all-to-all-done.1 = bf16[12,768,128]{2,1,0:T(8,128)(2,1)} async-done(((bf16[12,768,128]{2,1,0:T(8,128)(2,1)}), bf16[12,768,128]{2,1,0:T(8,128)(2,1)}, u32[]{:S(2)}, u32[]{:S(2)}) %all-to-all-start.1) | async-done | bytes 2359328 | tf_op jit(solution)/shard_map/all_to_all | solution.py:21
  34.1 48.1 %all_to_all.38 = bf16[192,2,32,128]{3,2,1,0:T(8,128)(2,1)S(1)} all-to-all(bf16[192,2,32,128]{3,2,1,0:T(8,128)(2,1)} %bitcast.32), channel_id=1, replica_groups=mesh['z'=4,'x'=4,'y'=4,'core'=2] {'z','x','y'}, dimensions={0} | all-to-all | bytes 6291456 | tf_op jit(solution)/shard_map/all_to_all | solution.py:18
  82.2 4.6 %fusion = bf16[2,3,768,16,32]{2,4,0,3,1:T(8,128)(2,1)S(1)} fusion(bf16[16,4,3,2,32,128]{5,4,3,2,1,0:T(8,128)(2,1)S(1)} %bitcast.36, bf16[4,3,768,128,1,1]{3,2,1,0,5,4:T(8,128)(2,1)} %bitcast.3), kind=kOutput, calls=%fused_computation.1 | convolution fusion | flops 2418278400 | bytes 10223616 | tf_op jit(solution)/shard_map/yjir,ayjcsr->cjias/dot_general | solution.py:23
  86.8 0.5 copy.28
  87.3 10.5 %all_to_all.39 = bf16[2,3,768,512]{2,3,1,0:T(8,128)(2,1)S(1)} all-to-all(bf16[2,3,768,512]{2,3,1,0:T(8,128)(2,1)S(1)} %bitcast.31), channel_id=1, replica_groups=mesh['z'=4,'x'=4,'y'=4,'core'=2] {'core'}, dimensions={0} | all-to-all | bytes 9437184 | tf_op jit(solution)/shard_map/all_to_all | solution.py:25
  97.7 1.9 add_convert_fusion
  99.7 4.3 %copy.29 = bf16[1,3,768,512]{3,2,1,0:T(8,128)(2,1)} copy(bf16[1,3,768,512]{2,3,1,0:T(8,128)(2,1)} %add_convert_fusion) | data formatting | bytes 4718592 | tf_op jit(solution)/shard_map/convert_element_type | solution.py:26
  104.0 5.0 %convert_element_type.38 = bf16[3,128,6,512]{3,2,1,0:T(8,128)(2,1)} reshape(bf16[1,3,768,512]{3,2,1,0:T(8,128)(2,1)} %copy.29) | data formatting | bytes 4718592 | tf_op jit(solution)/shard_map/convert_element_type | solution.py:26
  109.0 3.8 %copy.30 = bf16[128,6,3,512]{3,1,2,0:T(8,128)(2,1)} copy(bf16[128,6,3,512]{3,1,0,2:T(8,128)(2,1)} %bitcast.33) | data formatting | bytes 4718592 | tf_op jit(solution)/shard_map/transpose | solution.py:30
  112.8 0.0 copy-start.3
  112.8 0.0 copy-start.4
  112.8 0.0 copy-start.1
  112.8 0.0 copy-start.2
  112.8 5.0 %all-to-all-start.3 = ((bf16[128,6,3,512]{3,1,2,0:T(8,128)(2,1)}), bf16[128,6,3,512]{3,1,2,0:T(8,128)(2,1)}, u32[]{:S(2)}, u32[]{:S(2)}) async-start(bf16[128,6,3,512]{3,1,2,0:T(8,128)(2,1)} %copy.30), calls=%async_computation.3 | async-start | bytes 6291456 | tf_op jit(solution)/shard_map/all_to_all | solution.py:31
  117.9 0.0 copy-done.3
  117.9 0.0 copy-done.4
  117.9 0.1 broadcast_compare_fusion
  118.0 0.2 broadcast_in_dim.20
  118.2 0.4 broadcast_in_dim.21
  118.6 0.0 copy-done.1
  118.6 0.0 copy-done.2
  118.6 40.7 %all-to-all-done.3 = bf16[128,6,3,512]{3,1,2,0:T(8,128)(2,1)} async-done(((bf16[128,6,3,512]{3,1,2,0:T(8,128)(2,1)}), bf16[128,6,3,512]{3,1,2,0:T(8,128)(2,1)}, u32[]{:S(2)}, u32[]{:S(2)}) %all-to-all-start.3) | async-done | bytes 2359328 | tf_op jit(solution)/shard_map/all_to_all | solution.py:31
  159.3 5.1 %copy.50 = bf16[64,2,6,3,512]{4,1,3,0,2:T(2,128)(2,1)} copy(bf16[64,2,6,3,512]{4,2,3,1,0:T(8,128)(2,1)} %bitcast.9) | data formatting | bytes 4718592 | tf_op jit(solution)/shard_map/transpose | solution.py:32
  164.5 6.1 %reshape.57 = bf16[6,384,512]{2,1,0:T(8,128)(2,1)} reshape(bf16[6,64,3,2,512]{4,3,2,1,0:T(2,128)(2,1)} %bitcast.35) | data formatting | bytes 4718592 | tf_op jit(solution)/shard_map/reshape | solution.py:33
  170.6 0.0 copy-done
  170.6 5.2 %convert_bitcast_fusion = bf16[6,512,384]{1,2,0:T(8,128)(2,1)} fusion(bf16[6,512,512]{2,1,0:T(8,128)(2,1)S(1)} %copy-done, f32[6,512]{1,0:T(8,128)S(1)} %add_divide_fusion, bf16[6,384,512]{2,1,0:T(8,128)(2,1)} %reshape.57, pred[6,384]{1,0:T(8,128)(4,1)S(1)} %broadcast_in_dim.21), kind=kOutput, calls=%fused_computation.9 | convolution fusion | flops 2420637696 | bytes 7878912 | tf_op jit(solution)/shard_map/iks,ikj->isj/dot_general | solution.py:40
  175.8 4.8 %copy.33 = bf16[6,512,384]{2,0,1:T(8,128)(2,1)} copy(bf16[6,512,384]{1,2,0:T(8,128)(2,1)} %convert_bitcast_fusion) | data formatting | bytes 4718592 | tf_op jit(solution)/shard_map/convert_element_type | solution.py:41
  180.6 42.0 %all_to_all.40 = bf16[6,512,384]{2,0,1:T(8,128)(2,1)S(1)} all-to-all(bf16[6,512,384]{2,0,1:T(8,128)(2,1)} %copy.33), channel_id=1, replica_groups=mesh['z'=4,'x'=4,'y'=4,'core'=2] {'y','core'}, dimensions={1} | all-to-all | bytes 4718592 | tf_op jit(solution)/shard_map/all_to_all | solution.py:41
  222.6 1.9 copy.35
  (1 shorter events, 0.0 us)
Async XLA Ops:
  0.0 170.6 %copy-start = (bf16[6,512,512]{2,1,0:T(8,128)(2,1)S(1)}, bf16[6,512,512]{2,1,0:T(8,128)(2,1)}, u32[]{:S(2)}) copy-start(bf16[6,512,512]{2,1,0:T(8,128)(2,1)} %param.11) | copy-start | bytes 9437188
  0.0 34.1 %all-to-all-start.1 = ((bf16[12,768,128]{2,1,0:T(8,128)(2,1)}), bf16[12,768,128]{2,1,0:T(8,128)(2,1)}, u32[]{:S(2)}, u32[]{:S(2)}) async-start(bf16[12,768,128]{2,1,0:T(8,128)(2,1)} %param.8), calls=%async_computation.1 | async-start | bytes 4718592 | tf_op jit(solution)/shard_map/all_to_all | solution.py:21
  112.8 5.0 %copy-start.3 = (s32[192]{0:T(256)S(1)}, s32[192]{0:T(256)}, u32[]{:S(2)}) copy-start(s32[192]{0:T(256)} %param.9) | copy-start | bytes 2308
  112.8 5.0 %copy-start.4 = (s32[6]{0:T(128)S(1)}, s32[6]{0:T(128)}, u32[]{:S(2)}) copy-start(s32[6]{0:T(128)} %param.10) | copy-start | bytes 76
  112.8 5.8 %copy-start.1 = (f32[6,512]{1,0:T(8,128)S(1)}, f32[6,512]{1,0:T(8,128)}, u32[]{:S(2)}) copy-start(f32[6,512]{1,0:T(8,128)} %param.12) | copy-start | bytes 36868
  112.8 5.8 %copy-start.2 = (f32[6,512]{1,0:T(8,128)S(1)}, f32[6,512]{1,0:T(8,128)}, u32[]{:S(2)}) copy-start(f32[6,512]{1,0:T(8,128)} %param.13) | copy-start | bytes 36868
  112.8 46.5 %all-to-all-start.3 = ((bf16[128,6,3,512]{3,1,2,0:T(8,128)(2,1)}), bf16[128,6,3,512]{3,1,2,0:T(8,128)(2,1)}, u32[]{:S(2)}, u32[]{:S(2)}) async-start(bf16[128,6,3,512]{3,1,2,0:T(8,128)(2,1)} %copy.30), calls=%async_computation.3 | async-start | bytes 6291456 | tf_op jit(solution)/shard_map/all_to_all | solution.py:31
where the time goes:
time: 226 us; the launch traced here: 224 us
  blocking collectives  101 us (45%)
  waiting for transfers between devices  64 us (28%)
  local copies, waits for them, and re-layouts  37.8 us (17%)
  starting transfers between devices  10.3 us (5%)
  matrix products  9.76 us (4%)
    all_to_all x1, blocking collectives, body(): f = lax.all_to_all(f, PLANE, split_axis=0, concat_axis=0, tiled=True)  48.1 us
    all_to_all x1, blocking collectives, body(): lax.all_to_all(out.astype(jnp.bfloat16), BLK, split_axis=1, concat_axis=0...  42 us
    all_to_all x1, waiting for transfers between devices, body(): c = lax.all_to_all(c, ALL, split_axis=0, concat_axis=0, tiled=True)  40.7 us
    all_to_all x1, waiting for transfers between devices, body(): t = lax.all_to_all(legendre, 'y', split_axis=0, concat_axis=0, tiled=True)  23.3 us
    all_to_all x1, blocking collectives, body(): both = lax.all_to_all(part, 'core', split_axis=0, concat_axis=0, tiled=True)  10.5 us
    convert_element_type x2, local copies, waits for them, and re-layouts, body(): (both[0].astype(jnp.float32) + both[1].astype(jnp.float32)).astype(jnp.bf...  9.36 us
    reshape x1, local copies, waits for them, and re-layouts, body(): coeffs = c.reshape(local, cols, 2, total)  6.12 us
    unnamed x11, local copies, waits for them, and re-layouts  5.57 us
  transfers between devices with their start and end apart: 2, of which 2 were waited for; matrix products, arithmetic and copies ran while one was open for 3% of the time, Pallas kernels for 0%

commit v1 on v0

--- a/solution.py
+++ b/solution.py
@@ -38,7 +38,12 @@
     wiener = signal_power / (signal_power + noise_power)
     scaled = (forward * wiener[:, :, None]).astype(jnp.bfloat16)
     out = jnp.einsum("iks,ikj->isj", bessel, scaled, preferred_element_type=jnp.float32)
-    return lax.all_to_all(out.astype(jnp.bfloat16), BLK, split_axis=1, concat_axis=0, tiled=True)
+    return jnp.concatenate(
+        lax.all_to_all(
+            jnp.stack(jnp.split(out.astype(jnp.bfloat16), lax.axis_size(BLK), axis=1)), BLK, 0, 0
+        ),
+        axis=0,
+    )
 
 
 def solution(mesh):

time: 226 us -> 229 us (1.013)
  local copies, waits for them, and re-layouts: 37.8 us -> 49.6 us
  blocking collectives: 101 us -> 92.1 us
    unnamed x11 -> x21, local copies, waits for them, and re-layouts: 5.57 us -> 17 us
    all_to_all x1, blocking collectives: 42 us -> 33.5 us  [body(): lax.all_to_all(jnp.stack(jnp.split(out.astype(jnp.bfloat16), lax.axis_siz...]
    another operation x0 -> x2, local copies, waits for them, and re-layouts: none -> 7.07 us  [body(): jnp.stack(jnp.split(out.astype(jnp.bfloat16), lax.axis_size(BLK), axis=1))]
    convert_element_type x1 -> x0, local copies, waits for them, and re-layouts: 4.8 us -> none  [body(): out.astype(jnp.bfloat16)]
where the time goes in v1:
time: 229 us; the launch traced here: 228 us
  blocking collectives  92.1 us (40%)
  waiting for transfers between devices  64 us (28%)
  local copies, waits for them, and re-layouts  49.6 us (22%)
  starting transfers between devices  10.3 us (4%)
  matrix products  9.76 us (4%)
    all_to_all x1, blocking collectives, body(): f = lax.all_to_all(f, PLANE, split_axis=0, concat_axis=0, tiled=True)  48.1 us
    all_to_all x1, waiting for transfers between devices, body(): c = lax.all_to_all(c, ALL, split_axis=0, concat_axis=0, tiled=True)  40.7 us
    all_to_all x1, blocking collectives, body(): lax.all_to_all(jnp.stack(jnp.split(out.astype(jnp.bfloat16), lax.axis_siz...  33.5 us
    all_to_all x1, waiting for transfers between devices, body(): t = lax.all_to_all(legendre, 'y', split_axis=0, concat_axis=0, tiled=True)  23.3 us
    unnamed x21, local copies, waits for them, and re-layouts  17 us
    all_to_all x1, blocking collectives, body(): both = lax.all_to_all(part, 'core', split_axis=0, concat_axis=0, tiled=True)  10.5 us
    convert_element_type x2, local copies, waits for them, and re-layouts, body(): (both[0].astype(jnp.float32) + both[1].astype(jnp.float32)).astype(jnp.bf...  9.35 us
    another operation x2, local copies, waits for them, and re-layouts, body(): jnp.stack(jnp.split(out.astype(jnp.bfloat16), lax.axis_size(BLK), axis=1))  7.07 us
  transfers between devices with their start and end apart: 2, of which 2 were waited for; matrix products, arithmetic and copies ran while one was open for 3% of the time, Pallas kernels for 0%

profile of v1, /device:TPU:1, one launch (start us, length us, event | category | flops | bytes accessed | tf_op | source)
XLA Modules:
  0.0 227.8 jit_solution(16882216143470103210)
XLA Ops:
  0.0 0.0 copy-start
  0.0 5.3 %all-to-all-start.1 = ((bf16[12,768,128]{2,1,0:T(8,128)(2,1)}), bf16[12,768,128]{2,1,0:T(8,128)(2,1)}, u32[]{:S(2)}, u32[]{:S(2)}) async-start(bf16[12,768,128]{2,1,0:T(8,128)(2,1)} %param.8), calls=%async_computation.1 | async-start | bytes 4718592 | tf_op jit(solution)/shard_map/all_to_all | solution.py:21
  5.3 5.5 %copy.45 = bf16[32,2,192,128]{3,0,1,2:T(8,128)(2,1)} copy(bf16[32,2,192,128]{3,2,1,0:T(8,128)(2,1)} %param.7) | data formatting | bytes 6291456 | tf_op args[0]
  10.8 23.3 %all-to-all-done.1 = bf16[12,768,128]{2,1,0:T(8,128)(2,1)} async-done(((bf16[12,768,128]{2,1,0:T(8,128)(2,1)}), bf16[12,768,128]{2,1,0:T(8,128)(2,1)}, u32[]{:S(2)}, u32[]{:S(2)}) %all-to-all-start.1) | async-done | bytes 2359328 | tf_op jit(solution)/shard_map/all_to_all | solution.py:21
  34.1 48.1 %all_to_all.25 = bf16[192,2,32,128]{3,2,1,0:T(8,128)(2,1)S(1)} all-to-all(bf16[192,2,32,128]{3,2,1,0:T(8,128)(2,1)} %bitcast.61), channel_id=1, replica_groups=mesh['z'=4,'x'=4,'y'=4,'core'=2] {'z','x','y'}, dimensions={0} | all-to-all | bytes 6291456 | tf_op jit(solution)/shard_map/all_to_all | solution.py:18
  82.2 4.6 %fusion = bf16[2,3,768,16,32]{2,4,0,3,1:T(8,128)(2,1)S(1)} fusion(bf16[16,4,3,2,32,128]{5,4,3,2,1,0:T(8,128)(2,1)S(1)} %bitcast.65, bf16[4,3,768,128,1,1]{3,2,1,0,5,4:T(8,128)(2,1)} %bitcast.3), kind=kOutput, calls=%fused_computation.1 | convolution fusion | flops 2418278400 | bytes 10223616 | tf_op jit(solution)/shard_map/yjir,ayjcsr->cjias/dot_general | solution.py:23
  86.8 0.5 copy.27
  87.3 10.5 %all_to_all.26 = bf16[2,3,768,512]{2,3,1,0:T(8,128)(2,1)S(1)} all-to-all(bf16[2,3,768,512]{2,3,1,0:T(8,128)(2,1)S(1)} %bitcast.60), channel_id=1, replica_groups=mesh['z'=4,'x'=4,'y'=4,'core'=2] {'core'}, dimensions={0} | all-to-all | bytes 9437184 | tf_op jit(solution)/shard_map/all_to_all | solution.py:25
  97.7 1.9 add_convert_fusion
  99.7 4.3 %copy.28 = bf16[1,3,768,512]{3,2,1,0:T(8,128)(2,1)} copy(bf16[1,3,768,512]{2,3,1,0:T(8,128)(2,1)} %add_convert_fusion) | data formatting | bytes 4718592 | tf_op jit(solution)/shard_map/convert_element_type | solution.py:26
  104.0 5.0 %convert_element_type.38 = bf16[3,128,6,512]{3,2,1,0:T(8,128)(2,1)} reshape(bf16[1,3,768,512]{3,2,1,0:T(8,128)(2,1)} %copy.28) | data formatting | bytes 4718592 | tf_op jit(solution)/shard_map/convert_element_type | solution.py:26
  109.0 3.8 %copy.29 = bf16[128,6,3,512]{3,1,2,0:T(8,128)(2,1)} copy(bf16[128,6,3,512]{3,1,0,2:T(8,128)(2,1)} %bitcast.62) | data formatting | bytes 4718592 | tf_op jit(solution)/shard_map/transpose | solution.py:30
  112.8 0.0 copy-start.4
  112.8 0.0 copy-start.5
  112.8 0.0 copy-start.2
  112.8 0.0 copy-start.3
  112.8 5.0 %all-to-all-start.3 = ((bf16[128,6,3,512]{3,1,2,0:T(8,128)(2,1)}), bf16[128,6,3,512]{3,1,2,0:T(8,128)(2,1)}, u32[]{:S(2)}, u32[]{:S(2)}) async-start(bf16[128,6,3,512]{3,1,2,0:T(8,128)(2,1)} %copy.29), calls=%async_computation.3 | async-start | bytes 6291456 | tf_op jit(solution)/shard_map/all_to_all | solution.py:31
  117.8 0.0 copy-done.4
  117.9 0.0 copy-done.5
  117.9 0.1 broadcast_compare_fusion
  117.9 0.2 broadcast_in_dim.20
  118.2 0.4 broadcast_in_dim.21
  118.6 0.0 copy-done.2
  118.6 0.0 copy-done.3
  118.6 40.7 %all-to-all-done.3 = bf16[128,6,3,512]{3,1,2,0:T(8,128)(2,1)} async-done(((bf16[128,6,3,512]{3,1,2,0:T(8,128)(2,1)}), bf16[128,6,3,512]{3,1,2,0:T(8,128)(2,1)}, u32[]{:S(2)}, u32[]{:S(2)}) %all-to-all-start.3) | async-done | bytes 2359328 | tf_op jit(solution)/shard_map/all_to_all | solution.py:31
  159.3 5.1 %copy.46 = bf16[64,2,6,3,512]{4,1,3,0,2:T(2,128)(2,1)} copy(bf16[64,2,6,3,512]{4,2,3,1,0:T(8,128)(2,1)} %bitcast.9) | data formatting | bytes 4718592 | tf_op jit(solution)/shard_map/transpose | solution.py:32
  164.4 6.1 %reshape.60 = bf16[6,384,512]{2,1,0:T(8,128)(2,1)} reshape(bf16[6,64,3,2,512]{4,3,2,1,0:T(2,128)(2,1)} %bitcast.64) | data formatting | bytes 4718592 | tf_op jit(solution)/shard_map/reshape | solution.py:33
  170.6 0.0 copy-done
  170.6 5.2 %convert_bitcast_fusion = bf16[6,512,384]{1,2,0:T(8,128)(2,1)} fusion(bf16[6,512,512]{2,1,0:T(8,128)(2,1)S(1)} %copy-done, f32[6,512]{1,0:T(8,128)S(1)} %add_divide_fusion, bf16[6,384,512]{2,1,0:T(8,128)(2,1)} %reshape.60, pred[6,384]{1,0:T(8,128)(4,1)S(1)} %broadcast_in_dim.21), kind=kOutput, calls=%fused_computation.9 | convolution fusion | flops 2420637696 | bytes 7878912 | tf_op jit(solution)/shard_map/iks,ikj->isj/dot_general | solution.py:40
  175.7 0.0 copy-start.1
  175.7 2.1 fusion.21
  177.8 2.1 fusion.20
  179.9 1.9 fusion.19
  181.9 0.0 copy-done.1
  181.9 1.0 fusion.18
  182.9 0.9 fusion.17
  183.8 1.0 fusion.16
  184.9 0.9 fusion.15
  185.8 1.1 fusion.14
  186.8 6.0 %copy.32 = bf16[8,6,64,384]{3,2,1,0:T(8,128)(2,1)} copy(bf16[8,6,64,384]{2,3,1,0:T(8,128)(2,1)} %fusion.14) | data formatting | bytes 4718592 | tf_op jit(solution)/shard_map/stack | solution.py:43
  192.9 33.5 %all_to_all.27 = bf16[8,6,64,384]{3,2,1,0:T(8,128)(2,1)S(1)} all-to-all(bf16[8,6,64,384]{3,2,1,0:T(8,128)(2,1)} %copy.32), channel_id=1, replica_groups=mesh['z'=4,'x'=4,'y'=4,'core'=2] {'y','core'}, dimensions={0} | all-to-all | bytes 4718592 | tf_op jit(solution)/shard_map/all_to_all | solution.py:42
  226.4 1.4 copy.55
  (1 shorter events, 0.0 us)
Async XLA Ops:
  0.0 170.6 %copy-start = (bf16[6,512,512]{2,1,0:T(8,128)(2,1)S(1)}, bf16[6,512,512]{2,1,0:T(8,128)(2,1)}, u32[]{:S(2)}) copy-start(bf16[6,512,512]{2,1,0:T(8,128)(2,1)} %param.11) | copy-start | bytes 9437188
  0.0 34.1 %all-to-all-start.1 = ((bf16[12,768,128]{2,1,0:T(8,128)(2,1)}), bf16[12,768,128]{2,1,0:T(8,128)(2,1)}, u32[]{:S(2)}, u32[]{:S(2)}) async-start(bf16[12,768,128]{2,1,0:T(8,128)(2,1)} %param.8), calls=%async_computation.1 | async-start | bytes 4718592 | tf_op jit(solution)/shard_map/all_to_all | solution.py:21
  112.8 5.0 %copy-start.4 = (s32[192]{0:T(256)S(1)}, s32[192]{0:T(256)}, u32[]{:S(2)}) copy-start(s32[192]{0:T(256)} %param.9) | copy-start | bytes 2308
  112.8 5.0 %copy-start.5 = (s32[6]{0:T(128)S(1)}, s32[6]{0:T(128)}, u32[]{:S(2)}) copy-start(s32[6]{0:T(128)} %param.10) | copy-start | bytes 76
  112.8 5.8 %copy-start.2 = (f32[6,512]{1,0:T(8,128)S(1)}, f32[6,512]{1,0:T(8,128)}, u32[]{:S(2)}) copy-start(f32[6,512]{1,0:T(8,128)} %param.12) | copy-start | bytes 36868
  112.8 5.8 %copy-start.3 = (f32[6,512]{1,0:T(8,128)S(1)}, f32[6,512]{1,0:T(8,128)}, u32[]{:S(2)}) copy-start(f32[6,512]{1,0:T(8,128)} %param.13) | copy-start | bytes 36868
  112.8 46.5 %all-to-all-start.3 = ((bf16[128,6,3,512]{3,1,2,0:T(8,128)(2,1)}), bf16[128,6,3,512]{3,1,2,0:T(8,128)(2,1)}, u32[]{:S(2)}, u32[]{:S(2)}) async-start(bf16[128,6,3,512]{3,1,2,0:T(8,128)(2,1)} %copy.29), calls=%async_computation.3 | async-start | bytes 6291456 | tf_op jit(solution)/shard_map/all_to_all | solution.py:31
  175.7 6.1 %copy-start.1 = (bf16[6,512,384]{1,2,0:T(8,128)(2,1)S(1)}, bf16[6,512,384]{1,2,0:T(8,128)(2,1)}, u32[]{:S(2)}) copy-start(bf16[6,512,384]{1,2,0:T(8,128)(2,1)} %convert_bitcast_fusion) | copy-start | bytes 7077892
